TPU v7x, 512 devices: a whole 4x8x8 slice. The times are simulated.
512 devices in a mesh: pipe: 32 (over z_lo, y, core), tensor: 16 (over z_hi, x).
Axes of the slice: x: 4, y: 8, z: 8 (z_hi: 4, z_lo: 2; z = z_hi * 2 + z_lo), core: 2. Of those that a mesh axis runs over, the one named last changes fastest.
Arguments:
- tokens: bfloat16 [256, 8192], P('pipe', 'tensor'), may hold values from -6 to 6
- gate_weight: bfloat16 [8192, 28672], P('tensor', 'pipe'), may hold values from -0.0625 to 0.0625
- upward_weight: bfloat16 [8192, 28672], P('tensor', 'pipe'), may hold values from -0.0625 to 0.0625
- down_weight: bfloat16 [28672, 8192], P('pipe', 'tensor'), may hold values from -0.03125 to 0.03125
- adapter_first_factors: bfloat16 [2, 8192, 64], P(None, 'tensor'), may hold values from -0.0625 to 0.0625
- adapter_second_factors: bfloat16 [2, 64, 28672], P(None, None, 'pipe'), may hold values from -0.75 to 0.75
- adapter_of_block: int32 [2], replicated, may hold values from 0 to 1, each once
- cotangent: bfloat16 [256, 8192], P('pipe', 'tensor'), may hold values from -6 to 6
Outputs:
- mixed: bfloat16 [256, 8192], P('pipe', 'tensor')
- grad_tokens: bfloat16 [256, 8192], P('pipe', 'tensor')
- grad_a: float32 [2, 8192, 64], P(None, 'tensor')
- grad_b: float32 [2, 64, 28672], P(None, None, 'pipe')
Inputs may be any that keep to these rules, and one draw needn't show every extreme that they name: `adapter_of_block`: each of the 2 adapters is named by exactly one block.
All inputs are finite; a program needn't handle non-finite values.
Results may differ from a plain program's by a relative error of at most 0.0052.
Values may be sent and summed in bfloat16 or wider, within the bound.
No kernel may reach another device: no remote copies, remote signals or barrier semaphores. Data moves between devices by JAX's collectives and lax.ppermute only.
A program may use at most 64 MiB of HBM per device.

v0:
```python
import jax
import jax.numpy as jnp
from jax import lax
from jax.sharding import PartitionSpec as P

BLOCK = 128
adapter_scale = 0.5


def adapter_mask(first_row, row_count, adapter_of_block, rank_columns):
    row_index = first_row + jnp.arange(row_count, dtype=jnp.int32)
    owner = row_index // BLOCK
    block_index = jnp.arange(adapter_of_block.shape[0], dtype=jnp.int32)
    chosen = jnp.sum(
        jnp.where(owner[:, None] == block_index[None, :], adapter_of_block[None, :], 0), axis=1
    )
    columns = jnp.arange(adapter_of_block.shape[0] * rank_columns, dtype=jnp.int32) // rank_columns
    return (columns[None, :] == chosen[:, None]).astype(jnp.float32)


def trailing_product(left, right):
    return lax.dot_general(
        left, right, (((1,), (1,)), ((), ())), preferred_element_type=jnp.float32
    )


def leading_product(left, right):
    return lax.dot_general(
        left, right, (((0,), (0,)), ((), ())), preferred_element_type=jnp.float32
    )


def on_device(
    tokens,
    gate_weight,
    upward_weight,
    down_weight,
    adapter_first_factors,
    adapter_second_factors,
    adapter_of_block,
    cotangent,
):
    adapter_total, width_shard, rank_columns = adapter_first_factors.shape
    hidden_shard = gate_weight.shape[1]
    first_factor_rows = jnp.transpose(adapter_first_factors, (1, 0, 2)).reshape(
        width_shard, adapter_total * rank_columns
    )
    second_factor_rows = adapter_second_factors.reshape(adapter_total * rank_columns, hidden_shard)
    pipe_rows = tokens.shape[0]
    all_rows = pipe_rows * lax.axis_size("pipe")
    tensor_rows = all_rows // lax.axis_size("tensor")
    token_rows = lax.all_gather(tokens, "pipe", axis=0, tiled=True)
    piece = token_rows
    parts = lax.psum_scatter(
        jnp.concatenate(
            [
                jnp.dot(piece, gate_weight, preferred_element_type=jnp.float32),
                jnp.dot(piece, upward_weight, preferred_element_type=jnp.float32),
                jnp.dot(piece, first_factor_rows, preferred_element_type=jnp.float32),
            ],
            axis=1,
        ),
        "tensor",
        scatter_dimension=0,
        tiled=True,
    )
    first_row = lax.axis_index("tensor") * tensor_rows
    adapter_select_mask = adapter_mask(first_row, parts.shape[0], adapter_of_block, rank_columns)
    gate = parts[:, :hidden_shard]
    upward_frozen_output = parts[:, hidden_shard : 2 * hidden_shard]
    reduced_activation = (parts[:, 2 * hidden_shard :] * adapter_select_mask).astype(jnp.bfloat16)
    upward_output = upward_frozen_output + adapter_scale * jnp.dot(
        reduced_activation, second_factor_rows, preferred_element_type=jnp.float32
    )
    sig = jax.nn.sigmoid(gate)
    act = gate * sig
    hidden = (act * upward_output).astype(jnp.bfloat16)
    hidden_all = lax.all_gather(hidden, "tensor", axis=0, tiled=True)
    piece = hidden_all
    mixed = lax.psum_scatter(
        jnp.dot(piece, down_weight, preferred_element_type=jnp.float32),
        "pipe",
        scatter_dimension=0,
        tiled=True,
    ).astype(jnp.bfloat16)
    adjoint_rows = lax.all_gather(cotangent, "pipe", axis=0, tiled=True)
    piece = adjoint_rows
    grad_hidden = lax.psum_scatter(
        trailing_product(piece, down_weight), "tensor", scatter_dimension=0, tiled=True
    )
    upward_gradient = (grad_hidden * act).astype(jnp.bfloat16)
    grad_gate = (grad_hidden * upward_output * sig * (1.0 + gate * (1.0 - sig))).astype(
        jnp.bfloat16
    )
    second_factor_term = adapter_scale * leading_product(reduced_activation, upward_gradient)
    second_factor_gradient = lax.psum(second_factor_term, "tensor")
    reduced_gradient = (
        adapter_scale * trailing_product(upward_gradient, second_factor_rows) * adapter_select_mask
    )
    low_summed = lax.psum(reduced_gradient, "pipe")
    low_all = lax.all_gather(low_summed, "tensor", axis=0, tiled=True)
    low_back = low_all.astype(jnp.bfloat16)
    stacked = jnp.concatenate([grad_gate, upward_gradient], axis=1)
    stacked_all = lax.all_gather(stacked, "tensor", axis=0, tiled=True)
    piece = stacked_all
    back_sum = lax.psum_scatter(
        trailing_product(piece[:, :hidden_shard], gate_weight)
        + trailing_product(piece[:, hidden_shard:], upward_weight),
        "pipe",
        scatter_dimension=0,
        tiled=True,
    )
    own_low = lax.dynamic_slice_in_dim(low_back, lax.axis_index("pipe") * pipe_rows, pipe_rows, 0)
    grad_tokens = (back_sum + trailing_product(own_low, first_factor_rows)).astype(jnp.bfloat16)
    grad_a_flat = leading_product(token_rows, low_back)
    grad_a = jnp.transpose(grad_a_flat.reshape(width_shard, adapter_total, rank_columns), (1, 0, 2))
    grad_b = second_factor_gradient.reshape(adapter_total, rank_columns, hidden_shard)
    return (mixed, grad_tokens, grad_a, grad_b)


def solution(mesh):
    in_specs = (
        P("pipe", "tensor"),
        P("tensor", "pipe"),
        P("tensor", "pipe"),
        P("pipe", "tensor"),
        P(None, "tensor", None),
        P(None, None, "pipe"),
        P(),
        P("pipe", "tensor"),
    )
    out_specs = (
        P("pipe", "tensor"),
        P("pipe", "tensor"),
        P(None, "tensor", None),
        P(None, None, "pipe"),
    )
    return jax.shard_map(
        on_device, mesh=mesh, in_specs=in_specs, out_specs=out_specs, check_vma=False
    )
```

profile of v0, /device:TPU:2, one launch (start us, length us, event | category | flops | bytes accessed | tf_op | source)
XLA Modules:
  0.0 687.5 jit_solution(7951810947184697650)
XLA Ops:
  7.2 0.0 copy-start
  7.2 0.0 copy-start.4
  7.2 0.0 copy-start.3
  7.2 0.0 reduce-scatter.9.cloned.1.call-start
  7.2 36.7 %all_gather.17 = bf16[256,512]{1,0:T(8,128)(2,1)S(1)} all-gather(bf16[8,512]{1,0:T(8,128)(2,1)} %param.15), channel_id=1, replica_groups=mesh['pipe'=32,'tensor'=16] {'pipe'}, dimensions={0}, use_global_device_ids=true | all-gather | bytes 270336 | tf_op jit(solution)/shard_map/all_gather | solution.py:86
  44.0 0.0 copy-done
  44.0 0.0 copy-start.1
  44.0 1.4 fusion.17
  45.4 0.0 copy-start.2
  45.4 0.0 reduce-scatter.9.cloned.1.call-update
  45.4 0.0 reduce-scatter.5.cloned.1.call-start
  45.5 0.0 copy-done.4
  45.5 31.6 %all_gather.15 = bf16[256,512]{1,0:T(8,128)(2,1)S(1)} all-gather(bf16[8,512]{1,0:T(8,128)(2,1)S(1)} %copy-done.4), channel_id=1, replica_groups=mesh['pipe'=32,'tensor'=16] {'pipe'}, dimensions={0}, use_global_device_ids=true | all-gather | bytes 270336 | tf_op jit(solution)/shard_map/all_gather | solution.py:52
  77.1 0.0 copy-done.3
  77.1 0.2 fusion.15
  77.3 0.0 copy-done.1
  77.3 0.4 fusion.13
  77.8 0.0 copy-done.2
  77.8 0.4 fusion.14
  78.2 1.4 pad_maximum_fusion
  79.6 0.0 reduce-scatter.5.cloned.1.call-update
  79.7 0.0 reduce-scatter.7.cloned.1.call-start
  79.8 0.5 copy-done.6
  80.3 0.1 fusion.9
  80.4 55.4 %reduce-scatter.9.cloned.1.call-done = f32[16,896]{1,0:T(8,128)} async-done(((f32[256,896]{1,0:T(8,128)}), f32[16,896]{1,0:T(8,128)}) %reduce-scatter.9.cloned.1.call-update) | async-done | bytes 57360 | tf_op jit(solution)/shard_map/reduce_scatter | solution.py:88
  135.8 96.3 %reduce-scatter.5.cloned.1.call-done = f32[16,1920]{1,0:T(8,128)} async-done(((f32[256,1920]{1,0:T(8,128)}), f32[16,1920]{1,0:T(8,128)}) %reduce-scatter.5.cloned.1.call-update) | async-done | bytes 122896 | tf_op jit(solution)/shard_map/reduce_scatter | solution.py:54
  232.0 0.0 copy-done.5
  232.0 1.1 multiply_convert_fusion.1
  233.1 43.2 %all_gather.16 = bf16[256,896]{1,0:T(8,128)(2,1)S(1)} all-gather(bf16[16,896]{1,0:T(8,128)(2,1)S(1)} %get-tuple-element.5), channel_id=1, replica_groups=mesh['pipe'=32,'tensor'=16] {'tensor'}, dimensions={0}, use_global_device_ids=true | all-gather | bytes 487424 | tf_op jit(solution)/shard_map/all_gather | solution.py:78
  276.3 1.2 fusion.16
  277.5 0.0 reduce-scatter.7.cloned.1.call-update
  277.6 0.0 reduce-scatter.11.cloned.1.call-start
  277.6 46.3 %all_gather.18 = bf16[256,1792]{1,0:T(8,128)(2,1)S(1)} all-gather(bf16[16,1792]{1,0:T(8,128)(2,1)S(1)} %pad_maximum_fusion.1), channel_id=1, replica_groups=mesh['pipe'=32,'tensor'=16] {'tensor'}, dimensions={0}, use_global_device_ids=true | all-gather | bytes 974848 | tf_op jit(solution)/shard_map/all_gather | solution.py:104
  323.9 0.5 fusion.4
  324.4 1.3 convolution_add_fusion
  325.6 0.0 reduce-scatter.11.cloned.1.call-update
  325.7 0.0 all-reduce.2.cloned.1.call-start
  325.7 0.2 fusion.2
  325.9 54.0 %psum.14 = bf16[16,128]{1,0:T(8,128)(2,1)S(1)} all-reduce(f32[16,128]{1,0:T(8,128)S(1)} %fusion.2), channel_id=1, replica_groups=mesh['pipe'=32,'tensor'=16] {'pipe'}, use_global_device_ids=true, to_apply=%region_5.6 | all-reduce | flops 2048 | bytes 12288 | tf_op jit(solution)/shard_map/psum | solution.py:100
  379.9 40.6 %all_gather.19 = bf16[256,128]{1,0:T(8,128)(2,1)S(1)} all-gather(bf16[16,128]{1,0:T(8,128)(2,1)S(1)} %psum.14), channel_id=1, replica_groups=mesh['pipe'=32,'tensor'=16] {'tensor'}, dimensions={0}, use_global_device_ids=true | all-gather | bytes 69632 | tf_op jit(solution)/shard_map/all_gather | solution.py:101
  420.5 1.8 convolution_multiply_fusion
  422.3 0.0 all-reduce.2.cloned.1.call-update
  422.4 0.9 fusion.18
  423.3 1.3 convert_element_type.24
  424.6 87.9 %reduce-scatter.11.cloned.1.call-done = f32[8,512]{1,0:T(8,128)} async-done(((f32[256,512]{1,0:T(8,128)}), f32[8,512]{1,0:T(8,128)}) %reduce-scatter.11.cloned.1.call-update) | async-done | bytes 16400 | tf_op jit(solution)/shard_map/reduce_scatter | solution.py:106
  512.5 1.4 fusion.1
  514.0 165.2 %all-reduce.2.cloned.1.call-done = f32[2,64,896]{2,1,0:T(8,128)} async-done(((f32[2,64,896]{2,1,0:T(8,128)}), f32[2,64,896]{2,1,0:T(8,128)}) %all-reduce.2.cloned.1.call-update) | async-done | bytes 458768 | tf_op jit(solution)/shard_map/psum | solution.py:96
  679.2 1.8 copy.16
  (6 shorter events, 0.0 us)
Async XLA Ops:
  7.2 36.8 %copy-start = (bf16[896,512]{1,0:T(8,128)(2,1)S(1)}, bf16[896,512]{1,0:T(8,128)(2,1)}, u32[]{:S(2)}) copy-start(bf16[896,512]{1,0:T(8,128)(2,1)} %param.11) | copy-start | bytes 2752516
  7.2 38.3 %copy-start.4 = (bf16[8,512]{1,0:T(8,128)(2,1)S(1)}, bf16[8,512]{1,0:T(8,128)(2,1)}, u32[]{:S(2)}) copy-start(bf16[8,512]{1,0:T(8,128)(2,1)} %param.8) | copy-start | bytes 24580
  7.2 69.9 %copy-start.3 = (bf16[2,512,64]{1,2,0:T(8,128)(2,1)S(1)}, bf16[2,512,64]{1,2,0:T(8,128)(2,1)}, u32[]{:S(2)}) copy-start(bf16[2,512,64]{1,2,0:T(8,128)(2,1)} %param.12) | copy-start | bytes 393220
  7.2 128.6 %reduce-scatter.9.cloned.1.call-start = ((), (), s32[]{:S(2)}) async-start(), calls=%async_computation.6 | async-start | bytes 974848 | tf_op jit(solution)/shard_map/reduce_scatter | solution.py:88
  44.0 33.3 %copy-start.1 = (bf16[512,896]{1,0:T(8,128)(2,1)S(1)}, bf16[512,896]{1,0:T(8,128)(2,1)}, u32[]{:S(2)}) copy-start(bf16[512,896]{1,0:T(8,128)(2,1)} %param.9) | copy-start | bytes 2752516
  45.4 32.4 %copy-start.2 = (bf16[512,896]{1,0:T(8,128)(2,1)S(1)}, bf16[512,896]{1,0:T(8,128)(2,1)}, u32[]{:S(2)}) copy-start(bf16[512,896]{1,0:T(8,128)(2,1)} %param.10) | copy-start | bytes 2752516
  45.4 186.6 %reduce-scatter.5.cloned.1.call-start = ((), (), s32[]{:S(2)}) async-start(), calls=%async_computation.4 | async-start | bytes 2088960 | tf_op jit(solution)/shard_map/reduce_scatter | solution.py:54
  79.6 0.7 copy-start.6
  79.6 152.4 %copy-start.5 = (bf16[2,64,896]{2,1,0:T(8,128)(2,1)S(1)}, bf16[2,64,896]{2,1,0:T(8,128)(2,1)}, u32[]{:S(2)}) copy-start(bf16[2,64,896]{2,1,0:T(8,128)(2,1)} %param.13) | copy-start | bytes 688132
  79.7 343.6 %reduce-scatter.7.cloned.1.call-start = ((), (), s32[]{:S(2)}) async-start(), calls=%async_computation.5 | async-start | bytes 540672 | tf_op jit(solution)/shard_map/reduce_scatter | solution.py:80
  277.6 234.9 %reduce-scatter.11.cloned.1.call-start = ((), (), s32[]{:S(2)}) async-start(), calls=%async_computation.7 | async-start | bytes 540672 | tf_op jit(solution)/shard_map/reduce_scatter | solution.py:106
  325.7 353.5 %all-reduce.2.cloned.1.call-start = ((), (), s32[]{:S(2)}) async-start(), calls=%async_computation.8 | async-start | bytes 917504 | tf_op jit(solution)/shard_map/psum | solution.py:96
Sparse Core Ops, SparseCore 0:
  45.5 90.1 reduce-scatter.8
  140.5 91.5 reduce-scatter.4
  277.7 117.5 reduce-scatter.6
  398.1 114.3 reduce-scatter.10
  515.8 163.2 all-reduce.1
where the time goes:
time: 688 us
  waiting for transfers between devices  405 us (59%)
  blocking collectives  252 us (37%)
  between operations  13.9 us (2%)
  matrix products  10.9 us (2%)
    psum x1, waiting for transfers between devices, on_device(): second_factor_gradient = lax.psum(second_factor_term, 'tensor')  165 us
    reduce_scatter x1, waiting for transfers between devices, on_device(): lax.psum_scatter(jnp.concatenate([jnp.dot(piece, gate_weight, preferred_e...  96.3 us
    reduce_scatter x1, waiting for transfers between devices, on_device(): lax.psum_scatter(trailing_product(piece[:, :hidden_shard], gate_weight) +...  87.9 us
    reduce_scatter x1, waiting for transfers between devices, on_device(): lax.psum_scatter(trailing_product(piece, down_weight), 'tensor', scatter_...  55.4 us
    psum x1, blocking collectives, on_device(): low_summed = lax.psum(reduced_gradient, 'pipe')  54 us
    all_gather x1, blocking collectives, on_device(): stacked_all = lax.all_gather(stacked, 'tensor', axis=0, tiled=True)  46.3 us
    all_gather x1, blocking collectives, on_device(): hidden_all = lax.all_gather(hidden, 'tensor', axis=0, tiled=True)  43.2 us
    all_gather x1, blocking collectives, on_device(): low_all = lax.all_gather(low_summed, 'tensor', axis=0, tiled=True)  40.6 us
  transfers between devices with their start and end apart: 5, of which 4 were waited for; matrix products, arithmetic and copies ran while one was open for 1% of the time, Pallas kernels for 0%

commit v1 on v0

--- a/solution.py
+++ b/solution.py
@@ -1,3 +1,4 @@
+import functools
 import jax
 import jax.numpy as jnp
 from jax import lax
@@ -5,6 +6,15 @@
 
 BLOCK = 128
 adapter_scale = 0.5
+
+
+def part_trees_on(sample, net_axis):
+    plain = lax.all_gather(sample, axis_name=net_axis)
+    piece_out = jnp.sum(plain, axis=0)
+    return piece_out
+
+
+wait_the_stops_all = functools.partial(part_trees_on, net_axis="tensor")
 
 
 def adapter_mask(first_row, row_count, adapter_of_block, rank_columns):
@@ -93,7 +103,7 @@
         jnp.bfloat16
     )
     second_factor_term = adapter_scale * leading_product(reduced_activation, upward_gradient)
-    second_factor_gradient = lax.psum(second_factor_term, "tensor")
+    second_factor_gradient = wait_the_stops_all(second_factor_term)
     reduced_gradient = (
         adapter_scale * trailing_product(upward_gradient, second_factor_rows) * adapter_select_mask
     )

time: 688 us -> 636 us (0.924)
  the two profiles are of different devices: /device:TPU:2 before, /device:TPU:1 now
where the time goes in v1:
time: 636 us
  waiting for transfers between devices  355 us (56%)
  blocking collectives  249 us (39%)
  between operations  13.9 us (2%)
  matrix products  10.9 us (2%)
  other arithmetic  7.08 us (1%)
    all_gather x1, waiting for transfers between devices, part_trees_on(): plain = lax.all_gather(sample, axis_name=net_axis)  113 us
    reduce_scatter x1, waiting for transfers between devices, on_device(): lax.psum_scatter(jnp.concatenate([jnp.dot(piece, gate_weight, preferred_e...  97.4 us
    reduce_scatter x1, waiting for transfers between devices, on_device(): lax.psum_scatter(trailing_product(piece[:, :hidden_shard], gate_weight) +...  91.9 us
    psum x1, blocking collectives, on_device(): low_summed = lax.psum(reduced_gradient, 'pipe')  66.5 us
    reduce_scatter x1, waiting for transfers between devices, on_device(): lax.psum_scatter(trailing_product(piece, down_weight), 'tensor', scatter_...  51.8 us
    all_gather x1, blocking collectives, on_device(): stacked_all = lax.all_gather(stacked, 'tensor', axis=0, tiled=True)  41.4 us
    all_gather x1, blocking collectives, on_device(): adjoint_rows = lax.all_gather(cotangent, 'pipe', axis=0, tiled=True)  38.2 us
    all_gather x1, blocking collectives, on_device(): hidden_all = lax.all_gather(hidden, 'tensor', axis=0, tiled=True)  37.6 us
  transfers between devices with their start and end apart: 5, of which 4 were waited for; matrix products, arithmetic and copies ran while one was open for 2% of the time, Pallas kernels for 0%

profile of v1, /device:TPU:1, one launch (start us, length us, event | category | flops | bytes accessed | tf_op | source)
XLA Modules:
  0.0 635.7 jit_solution(13800165477685143225)
XLA Ops:
  7.2 0.0 copy-start
  7.2 0.0 copy-start.4
  7.2 0.0 copy-start.3
  7.2 0.0 reduce-scatter.9.cloned.1.call-start
  7.2 38.2 %all_gather.23 = bf16[256,512]{1,0:T(8,128)(2,1)S(1)} all-gather(bf16[8,512]{1,0:T(8,128)(2,1)} %param.15), channel_id=1, replica_groups=mesh['pipe'=32,'tensor'=16] {'pipe'}, dimensions={0}, use_global_device_ids=true | all-gather | bytes 270336 | tf_op jit(solution)/shard_map/all_gather | solution.py:96
  45.5 0.0 copy-done
  45.5 0.0 copy-start.2
  45.5 1.4 fusion.17
  46.9 0.0 copy-start.1
  46.9 0.0 reduce-scatter.9.cloned.1.call-update
  46.9 0.0 reduce-scatter.5.cloned.1.call-start
  47.0 0.0 copy-done.4
  47.0 33.1 %all_gather.21 = bf16[256,512]{1,0:T(8,128)(2,1)S(1)} all-gather(bf16[8,512]{1,0:T(8,128)(2,1)S(1)} %copy-done.4), channel_id=1, replica_groups=mesh['pipe'=32,'tensor'=16] {'pipe'}, dimensions={0}, use_global_device_ids=true | all-gather | bytes 270336 | tf_op jit(solution)/shard_map/all_gather | solution.py:62
  80.1 0.0 copy-done.3
  80.1 0.2 fusion.15
  80.4 0.0 copy-done.2
  80.4 0.4 fusion.14
  80.8 0.0 copy-done.1
  80.8 0.4 fusion.13
  81.3 1.4 pad_maximum_fusion
  82.7 0.0 reduce-scatter.5.cloned.1.call-update
  82.7 0.0 reduce-scatter.7.cloned.1.call-start
  82.8 0.5 copy-done.6
  83.4 0.1 fusion.9
  83.4 51.8 %reduce-scatter.9.cloned.1.call-done = f32[16,896]{1,0:T(8,128)} async-done(((f32[256,896]{1,0:T(8,128)}), f32[16,896]{1,0:T(8,128)}) %reduce-scatter.9.cloned.1.call-update) | async-done | bytes 57360 | tf_op jit(solution)/shard_map/reduce_scatter | solution.py:98
  135.3 97.4 %reduce-scatter.5.cloned.1.call-done = f32[16,1920]{1,0:T(8,128)} async-done(((f32[256,1920]{1,0:T(8,128)}), f32[16,1920]{1,0:T(8,128)}) %reduce-scatter.5.cloned.1.call-update) | async-done | bytes 122896 | tf_op jit(solution)/shard_map/reduce_scatter | solution.py:64
  232.7 0.0 copy-done.5
  232.7 1.1 multiply_convert_fusion.1
  233.8 37.6 %all_gather.22 = bf16[256,896]{1,0:T(8,128)(2,1)S(1)} all-gather(bf16[16,896]{1,0:T(8,128)(2,1)S(1)} %get-tuple-element.5), channel_id=1, replica_groups=mesh['pipe'=32,'tensor'=16] {'tensor'}, dimensions={0}, use_global_device_ids=true | all-gather | bytes 487424 | tf_op jit(solution)/shard_map/all_gather | solution.py:88
  271.4 1.2 fusion.16
  272.6 0.0 reduce-scatter.7.cloned.1.call-update
  272.6 0.0 reduce-scatter.11.cloned.1.call-start
  272.7 41.4 %all_gather.24 = bf16[256,1792]{1,0:T(8,128)(2,1)S(1)} all-gather(bf16[16,1792]{1,0:T(8,128)(2,1)S(1)} %pad_maximum_fusion.1), channel_id=1, replica_groups=mesh['pipe'=32,'tensor'=16] {'tensor'}, dimensions={0}, use_global_device_ids=true | all-gather | bytes 974848 | tf_op jit(solution)/shard_map/all_gather | solution.py:114
  314.1 0.5 fusion.4
  314.6 1.3 convolution_add_fusion
  315.9 0.0 reduce-scatter.11.cloned.1.call-update
  315.9 0.0 all-gather.3.cloned.1.call-start
  316.0 1.8 convolution_multiply_fusion
  317.8 0.0 all-gather.3.cloned.1.call-update
  317.8 0.2 fusion.2
  318.0 66.5 %psum.7 = bf16[16,128]{1,0:T(8,128)(2,1)S(1)} all-reduce(f32[16,128]{1,0:T(8,128)S(1)} %fusion.2), channel_id=1, replica_groups=mesh['pipe'=32,'tensor'=16] {'pipe'}, use_global_device_ids=true, to_apply=%region_5.6 | all-reduce | flops 2048 | bytes 12288 | tf_op jit(solution)/shard_map/psum | solution.py:110
  384.5 31.7 %all_gather.25 = bf16[256,128]{1,0:T(8,128)(2,1)S(1)} all-gather(bf16[16,128]{1,0:T(8,128)(2,1)S(1)} %psum.7), channel_id=1, replica_groups=mesh['pipe'=32,'tensor'=16] {'tensor'}, dimensions={0}, use_global_device_ids=true | all-gather | bytes 69632 | tf_op jit(solution)/shard_map/all_gather | solution.py:111
  416.1 0.9 fusion.18
  417.0 1.3 convert_element_type.24
  418.4 91.9 %reduce-scatter.11.cloned.1.call-done = f32[8,512]{1,0:T(8,128)} async-done(((f32[256,512]{1,0:T(8,128)}), f32[8,512]{1,0:T(8,128)}) %reduce-scatter.11.cloned.1.call-update) | async-done | bytes 16400 | tf_op jit(solution)/shard_map/reduce_scatter | solution.py:116
  510.3 1.4 fusion.1
  511.7 113.3 %all-gather.3.cloned.1.call-done = f32[2048,896]{1,0:T(8,128)} async-done(((f32[128,896]{1,0:T(8,128)}), f32[2048,896]{1,0:T(8,128)}) %all-gather.3.cloned.1.call-update) | async-done | bytes 7340048 | tf_op jit(solution)/shard_map/all_gather | solution.py:12
  625.0 4.2 reduce_sum.19
  (6 shorter events, 0.0 us)
Async XLA Ops:
  7.2 38.3 %copy-start = (bf16[896,512]{1,0:T(8,128)(2,1)S(1)}, bf16[896,512]{1,0:T(8,128)(2,1)}, u32[]{:S(2)}) copy-start(bf16[896,512]{1,0:T(8,128)(2,1)} %param.11) | copy-start | bytes 2752516
  7.2 39.8 %copy-start.4 = (bf16[8,512]{1,0:T(8,128)(2,1)S(1)}, bf16[8,512]{1,0:T(8,128)(2,1)}, u32[]{:S(2)}) copy-start(bf16[8,512]{1,0:T(8,128)(2,1)} %param.8) | copy-start | bytes 24580
  7.2 72.9 %copy-start.3 = (bf16[2,512,64]{1,2,0:T(8,128)(2,1)S(1)}, bf16[2,512,64]{1,2,0:T(8,128)(2,1)}, u32[]{:S(2)}) copy-start(bf16[2,512,64]{1,2,0:T(8,128)(2,1)} %param.12) | copy-start | bytes 393220
  7.2 128.1 %reduce-scatter.9.cloned.1.call-start = ((), (), s32[]{:S(2)}) async-start(), calls=%async_computation.6 | async-start | bytes 974848 | tf_op jit(solution)/shard_map/reduce_scatter | solution.py:98
  45.5 34.9 %copy-start.2 = (bf16[512,896]{1,0:T(8,128)(2,1)S(1)}, bf16[512,896]{1,0:T(8,128)(2,1)}, u32[]{:S(2)}) copy-start(bf16[512,896]{1,0:T(8,128)(2,1)} %param.10) | copy-start | bytes 2752516
  46.9 33.9 %copy-start.1 = (bf16[512,896]{1,0:T(8,128)(2,1)S(1)}, bf16[512,896]{1,0:T(8,128)(2,1)}, u32[]{:S(2)}) copy-start(bf16[512,896]{1,0:T(8,128)(2,1)} %param.9) | copy-start | bytes 2752516
  46.9 185.7 %reduce-scatter.5.cloned.1.call-start = ((), (), s32[]{:S(2)}) async-start(), calls=%async_computation.4 | async-start | bytes 2088960 | tf_op jit(solution)/shard_map/reduce_scatter | solution.py:64
  82.7 0.7 copy-start.6
  82.7 150.0 %copy-start.5 = (bf16[2,64,896]{2,1,0:T(8,128)(2,1)S(1)}, bf16[2,64,896]{2,1,0:T(8,128)(2,1)}, u32[]{:S(2)}) copy-start(bf16[2,64,896]{2,1,0:T(8,128)(2,1)} %param.13) | copy-start | bytes 688132
  82.7 334.3 %reduce-scatter.7.cloned.1.call-start = ((), (), s32[]{:S(2)}) async-start(), calls=%async_computation.5 | async-start | bytes 540672 | tf_op jit(solution)/shard_map/reduce_scatter | solution.py:90
  272.6 237.6 %reduce-scatter.11.cloned.1.call-start = ((), (), s32[]{:S(2)}) async-start(), calls=%async_computation.7 | async-start | bytes 540672 | tf_op jit(solution)/shard_map/reduce_scatter | solution.py:116
  315.9 309.0 %all-gather.3.cloned.1.call-start = ((), (), s32[]{:S(2)}) async-start(), calls=%async_computation.8 | async-start | bytes 7798784 | tf_op jit(solution)/shard_map/all_gather | solution.py:12
Sparse Core Ops, SparseCore 0:
  47.1 88.1 reduce-scatter.8
  140.0 92.6 reduce-scatter.4
  272.8 121.1 reduce-scatter.6
  396.8 113.4 reduce-scatter.10
  513.7 111.2 all-gather.2
